TPU v7x, 32 devices: a whole 2x2x4 slice. The times are simulated.
32 devices in a mesh: row: 4 (over y, core), col: 8 (over z, x).
Axes of the slice: x: 2, y: 2, z: 4, core: 2. Of those that a mesh axis runs over, the one named last changes fastest.
Arguments:
- ancestor_inverse: float32 [1024, 1024], P('row', 'col'), may hold values from -6 to 6
- pattern: int32 [8, 8], replicated, may hold values 0 or 1
- listed: int32 [2, 4], replicated, may hold values from 0 to 7, as said below
- panels: float32 [2, 1024, 512], P(None, ('col', 'row')), may hold values from -0.1875 to 0.1875
- parent_panels: float32 [1, 512, 512], replicated, may hold values from -0.25 to 0.25
- diag_inverse: float32 [2, 512, 512], P(None, 'row', 'col'), may hold values from -6 to 6
Outputs:
- upper_blocks: float32 [2, 1024, 512], P(None, ('col', 'row'))
- diagonal_blocks: float32 [2, 512, 512], P(None, 'row', 'col')
Inputs may be any that keep to these rules, and one draw needn't show every extreme that they name: Each row of listed names 4 different blocks.
All inputs are finite; a program needn't handle non-finite values.
Results may differ from a plain program's by a relative error of at most 0.00011.
Values sent between devices are 32-bit elements; how exact they have to be, the bound alone decides.
No kernel may reach another device: no remote copies, remote signals or barrier semaphores. Data moves between devices by JAX's collectives and lax.ppermute only.
A program may use at most 64 MiB of HBM per device.

v0:
```python
import jax
import jax.numpy as jnp
from jax import lax
from jax.sharding import PartitionSpec as P

BLK = 128


def broadcast(value, axis, source):
    kept = jnp.where(lax.axis_index(axis) == source, value, 0).astype(value.dtype)
    return lax.psum(kept, axis)


def contract_rows(left, right):
    return lax.dot_general(
        left,
        right,
        (((0,), (0,)), ((), ())),
        precision=lax.Precision.HIGHEST,
        preferred_element_type=jnp.float32,
    )


def local(ancestor_inverse, pattern, listed, panels, parent_panels, diag_inverse):
    highest = lax.Precision.HIGHEST
    rows_here, cols_here = ancestor_inverse.shape
    row_count = lax.axis_size("row")
    col_count = lax.axis_size("col")
    column_ratio = col_count // row_count
    row_index = lax.axis_index("row")
    col_index = lax.axis_index("col")
    super_count, shard_rows, panel_width = panels.shape
    row_tiles = rows_here // BLK
    col_tiles = cols_here // BLK
    blocks = pattern.shape[0]
    tile_mask = lax.dynamic_slice(
        pattern, (row_index * row_tiles, col_index * col_tiles), (row_tiles, col_tiles)
    ).astype(jnp.float32)
    masked = (
        ancestor_inverse.reshape(row_tiles, BLK, col_tiles, BLK) * tile_mask[:, None, :, None]
    ).reshape(rows_here, cols_here)
    block_ids = jnp.arange(blocks, dtype=jnp.int32)
    listed_flags = jnp.any(listed[:, :, None] == block_ids[None, None, :], axis=1).astype(
        jnp.float32
    )
    first_row = (col_index * row_count + row_index) * shard_rows
    shard_blocks = (first_row + jnp.arange(shard_rows, dtype=jnp.int32)) // BLK
    onehot = (shard_blocks[:, None] == block_ids[None, :]).astype(jnp.float32)
    row_keep = jnp.dot(
        listed_flags, onehot.T, precision=highest, preferred_element_type=jnp.float32
    )
    kept_panels = panels * row_keep[:, :, None]
    tile_rows = panel_width // row_count
    tile_cols = panel_width // col_count
    column_slabs = lax.all_gather(kept_panels, "row", axis=1, tiled=True)
    received = [
        broadcast(column_slabs, "col", column_ratio * row_index + member)
        for member in range(column_ratio)
    ]
    all_slabs = jnp.concatenate(received, axis=1)
    uppers = []
    diagonals = []
    previous_upper = None
    previous_tile = None
    for supernode in range(super_count):
        row_slab = all_slabs[supernode]
        column_sum = lax.psum_scatter(
            contract_rows(masked, row_slab), "row", scatter_dimension=0, tiled=True
        )
        if supernode > 0:
            parent_link = parent_panels[supernode - 1]
            chained = jnp.dot(
                previous_upper, parent_link, precision=highest, preferred_element_type=jnp.float32
            )
            column_sum = column_sum + chained
        upper_part = -column_sum * row_keep[supernode][:, None]
        partial_value = -contract_rows(kept_panels[supernode], upper_part)
        if supernode > 0:
            partial_value = partial_value + contract_rows(chained, kept_panels[supernode])
            link_band = lax.dynamic_slice_in_dim(parent_link, row_index * tile_rows, tile_rows, 0)
            link_slice = lax.dynamic_slice_in_dim(parent_link, col_index * tile_cols, tile_cols, 0)
            inner = jnp.dot(
                previous_tile, link_slice, precision=highest, preferred_element_type=jnp.float32
            )
            partial_value = partial_value + contract_rows(link_band, inner)
        partial_value = lax.dynamic_update_slice(
            partial_value,
            lax.dynamic_slice(
                partial_value,
                (row_index * tile_rows, col_index * tile_cols),
                (tile_rows, tile_cols),
            )
            + diag_inverse[supernode],
            (row_index * tile_rows, col_index * tile_cols),
        )
        row_band = lax.psum_scatter(partial_value, "row", scatter_dimension=0, tiled=True)
        diag_tile = lax.psum_scatter(row_band, "col", scatter_dimension=1, tiled=True)
        previous_upper = upper_part
        previous_tile = diag_tile
        uppers.append(upper_part)
        diagonals.append(diag_tile)
    return (jnp.stack(uppers), jnp.stack(diagonals))


def solution(mesh):
    return jax.shard_map(
        local,
        mesh=mesh,
        in_specs=(
            P("row", "col"),
            P(),
            P(),
            P(None, ("col", "row"), None),
            P(),
            P(None, "row", "col"),
        ),
        out_specs=(P(None, ("col", "row"), None), P(None, "row", "col")),
        check_vma=False,
    )
```

profile of v0, /device:TPU:0, one launch (start us, length us, event | category | flops | bytes accessed | tf_op | source)
XLA Modules:
  0.0 339.1 jit_solution(17373417434991625303)
XLA Ops:
  8.3 1.0 broadcast_multiply_fusion
  9.3 8.7 %all_gather.3 = f32[2,128,512]{2,1,0:T(8,128)S(1)} all-gather(f32[2,32,512]{2,1,0:T(8,128)S(1)} %broadcast_multiply_fusion), channel_id=1, replica_groups=mesh['row'=4,'col'=8] {'row'}, dimensions={1}, use_global_device_ids=true | all-gather | bytes 655360 | tf_op jit(solution)/shard_map/all_gather | solution.py:55
  17.9 1.2 broadcast_select_fusion
  19.2 0.9 convert_reduce_fusion
  20.1 78.2 %all-reduce.3.cloned.1.call-done = (f32[2,128,512]{2,1,0:T(8,128)}, f32[2,128,512]{2,1,0:T(8,128)}) async-done(((f32[2,128,512]{2,1,0:T(8,128)}, f32[2,128,512]{2,1,0:T(8,128)}), (f32[2,128,512]{2,1,0:T(8,128)}, f32[2,128,512]{2,1,0:T(8,128)})) %all-reduce.3.cloned.1.call-update) | async-done | bytes 1048592 | tf_op jit(solution)/shard_map/psum | solution.py:11
  98.4 1.1 constant_dynamic-update-slice_fusion.1
  99.6 0.9 copy-done.5
  100.5 1.2 fusion.4
  101.8 19.8 %reduce-scatter.7.cloned.1.call-done = f32[32,512]{1,0:T(8,128)} async-done(((f32[128,512]{1,0:T(8,128)}), f32[32,512]{1,0:T(8,128)}) %reduce-scatter.7.cloned.1.call-update) | async-done | bytes 65552 | tf_op jit(solution)/shard_map/reduce_scatter | solution.py:67
  121.5 2.0 convolution_negate_fusion.1
  123.5 1.0 copy-done.2
  124.6 1.2 fusion.3
  125.8 23.6 %reduce-scatter.11.cloned.1.call-done = f32[128,512]{0,1:T(8,128)} async-done(((f32[512,512]{0,1:T(8,128)}), f32[128,512]{0,1:T(8,128)}) %reduce-scatter.11.cloned.1.call-update) | async-done | bytes 262160 | tf_op jit(solution)/shard_map/reduce_scatter | solution.py:96
  149.5 0.8 copy-done.3
  151.0 20.8 %reduce-scatter.9.cloned.1.call-done = f32[32,512]{1,0:T(8,128)} async-done(((f32[128,512]{1,0:T(8,128)}), f32[32,512]{1,0:T(8,128)}) %reduce-scatter.9.cloned.1.call-update) | async-done | bytes 65552 | tf_op jit(solution)/shard_map/reduce_scatter | solution.py:67
  171.8 1.9 convolution_negate_fusion
  173.8 63.4 %reduce-scatter.13.cloned.1.call-done = f32[128,64]{0,1:T(8,128)} async-done(((f32[128,512]{0,1:T(8,128)}), f32[128,64]{0,1:T(8,128)}) %reduce-scatter.13.cloned.1.call-update) | async-done | bytes 32784 | tf_op jit(solution)/shard_map/reduce_scatter | solution.py:97
  237.1 1.2 fusion.8
  238.3 1.0 fusion.5
  239.3 1.1 fusion
  240.4 1.0 copy-done.1
  241.5 24.0 %reduce-scatter.15.cloned.1.call-done = f32[128,512]{0,1:T(8,128)} async-done(((f32[512,512]{0,1:T(8,128)}), f32[128,512]{0,1:T(8,128)}) %reduce-scatter.15.cloned.1.call-update) | async-done | bytes 262160 | tf_op jit(solution)/shard_map/reduce_scatter | solution.py:96
  267.0 63.8 %reduce-scatter.17.cloned.1.call-done = f32[128,64]{0,1:T(8,128)} async-done(((f32[128,512]{0,1:T(8,128)}), f32[128,64]{0,1:T(8,128)}) %reduce-scatter.17.cloned.1.call-update) | async-done | bytes 32784 | tf_op jit(solution)/shard_map/reduce_scatter | solution.py:97
  330.9 1.4 pad_maximum_fusion.1
  (42 shorter events, 4.0 us)
Async XLA Ops:
  7.2 142.4 %copy-start = (f32[1,512,512]{2,1,0:T(8,128)S(1)}, f32[1,512,512]{2,1,0:T(8,128)}, u32[]{:S(2)}) copy-start(f32[1,512,512]{2,1,0:T(8,128)} %param.10) | copy-start | bytes 3145732
  7.2 91.2 %all-reduce.3.cloned.1.call-start = ((), (), s32[]{:S(2)}) async-start(), calls=%async_computation.12 | async-start | bytes 2097152 | tf_op jit(solution)/shard_map/psum | solution.py:11
  7.2 0.8 copy-start.9
  19.1 102.4 %reduce-scatter.7.cloned.1.call-start = ((), (), s32[]{:S(2)}) async-start(), calls=%async_computation.6 | async-start | bytes 327680 | tf_op jit(solution)/shard_map/reduce_scatter | solution.py:67
  98.3 1.2 copy-start.4
  99.5 0.9 copy-start.5
  101.7 47.8 %reduce-scatter.11.cloned.1.call-start = ((), (), s32[]{:S(2)}) async-start(), calls=%async_computation.8 | async-start | bytes 1310720 | tf_op jit(solution)/shard_map/reduce_scatter | solution.py:96
  121.5 2.0 copy-start.8
  123.5 1.0 copy-start.2
  124.5 47.3 %reduce-scatter.9.cloned.1.call-start = ((), (), s32[]{:S(2)}) async-start(), calls=%async_computation.7 | async-start | bytes 327680 | tf_op jit(solution)/shard_map/reduce_scatter | solution.py:67
  125.8 111.3 %reduce-scatter.13.cloned.1.call-start = ((), (), s32[]{:S(2)}) async-start(), calls=%async_computation.9 | async-start | bytes 294912 | tf_op jit(solution)/shard_map/reduce_scatter | solution.py:97
  149.5 0.8 copy-start.3
  149.5 116.0 %reduce-scatter.15.cloned.1.call-start = ((), (), s32[]{:S(2)}) async-start(), calls=%async_computation.10 | async-start | bytes 1310720 | tf_op jit(solution)/shard_map/reduce_scatter | solution.py:96
  240.4 1.0 copy-start.1
  241.4 89.5 %reduce-scatter.17.cloned.1.call-start = ((), (), s32[]{:S(2)}) async-start(), calls=%async_computation.11 | async-start | bytes 294912 | tf_op jit(solution)/shard_map/reduce_scatter | solution.py:97
  265.5 0.8 copy-start.6
  266.4 64.5 %copy-start.7 = (f32[128,64]{0,1:T(8,128)S(1)}, f32[128,64]{0,1:T(8,128)}, u32[]{:S(2)}) copy-start(f32[128,64]{0,1:T(8,128)} %reduce-scatter.13.cloned.1.call-done) | copy-start | bytes 98308
Sparse Core Ops, SparseCore 0:
  19.2 79.0 all-reduce.2
  101.8 19.6 reduce-scatter.6
  124.6 24.7 reduce-scatter.10
  151.8 20.0 reduce-scatter.8
  175.0 62.0 reduce-scatter.12
  241.5 23.8 reduce-scatter.14
  268.8 62.0 reduce-scatter.16
where the time goes:
time: 340 us; the launch traced here: 339 us
  waiting for transfers between devices  294 us (86%)
  between operations  14.3 us (4%)
  matrix products  10.5 us (3%)
  blocking collectives  8.68 us (3%)
  local copies, waits for them, and re-layouts  6.36 us (2%)
  other arithmetic  5.36 us (2%)
    reduce_scatter x2, waiting for transfers between devices, local(): lax.psum_scatter(row_band, 'col', scatter_dimension=1, tiled=True)  127 us
    psum x1, waiting for transfers between devices, broadcast(): return lax.psum(kept, axis)  78.2 us
    reduce_scatter x2, waiting for transfers between devices, local(): lax.psum_scatter(partial_value, 'row', scatter_dimension=0, tiled=True)  47.6 us
    reduce_scatter x2, waiting for transfers between devices, local(): lax.psum_scatter(contract_rows(masked, row_slab), 'row', scatter_dimensio...  40.6 us
    all_gather x1, blocking collectives, local(): column_slabs = lax.all_gather(kept_panels, 'row', axis=1, tiled=True)  8.68 us
    dot_general x6, matrix products, contract_rows(): lax.dot_general(left, right, (((0,), (0,)), ((), ())), precision=lax.Prec...  8.39 us
  transfers between devices with their start and end apart: 7, of which 7 were waited for; matrix products, arithmetic and copies ran while one was open for 2% of the time, Pallas kernels for 0%

commit v1 on v0

v1 whole, which is shorter than its diff:
```python
import jax
import jax.numpy as jnp
from jax import lax
from jax.sharding import PartitionSpec as P


BLK = 128


def swap(value, row_step, col_step):
    rows = lax.axis_size("row")
    cols = lax.axis_size("col")
    if col_step == 0:
        return lax.ppermute(value, "row", [(i, i ^ row_step) for i in range(rows)])
    if row_step == 0:
        return lax.ppermute(value, "col", [(i, i ^ col_step) for i in range(cols)])
    pairs = [
        (row * cols + col, (row ^ row_step) * cols + (col ^ col_step))
        for row in range(rows)
        for col in range(cols)
    ]
    return lax.ppermute(value, ("row", "col"), pairs)


def join(parts, other):
    return jnp.stack([parts, other], axis=1).reshape((-1,) + parts.shape[1:])


def after(value, *others):
    return lax.optimization_barrier((value,) + others)[1:]


def direct_gather(value):
    rows = lax.axis_size("row")
    far = [[swap(value, j, k) if j or k else value for k in range(2)] for j in range(0, rows, 2)]
    far = jnp.stack([jnp.stack(pair) for pair in far])
    return join(far, swap(far, 1, 0))


def rows_first(value):
    rows = lax.axis_size("row")
    far = value[None]
    step = rows // 2
    while step > 1:
        far = join(far, swap(far, step, 0))
        step //= 2
    far = jnp.stack([far, swap(far, 0, 1)], axis=1)
    return join(far, swap(far, 1, 0))


def column_first(value):
    rows = lax.axis_size("row")
    far = jnp.stack([value, swap(value, 0, 1)])[None]
    step = rows // 2
    while step > 1:
        far = join(far, swap(far, step, 0))
        step //= 2
    return join(far, swap(far, 1, 0))


def pick(value, *index):
    sizes = (1,) * len(index) + value.shape[len(index) :]
    start = tuple(index) + (0,) * (value.ndim - len(index))
    return lax.dynamic_slice(value, start, sizes).reshape(value.shape[len(index) :])


def dot(left, right, left_dim=1, right_dim=0):
    return lax.dot_general(
        left,
        right,
        (((left_dim,), (right_dim,)), ((), ())),
        precision=lax.Precision.HIGH,
        preferred_element_type=jnp.float32,
    )


def local(ancestor_inverse, pattern, listed, panels, parent_panels, diag_inverse):
    rows_here, cols_here = ancestor_inverse.shape
    row_count = lax.axis_size("row")
    col_count = lax.axis_size("col")
    row_index = lax.axis_index("row")
    col_index = lax.axis_index("col")
    low = col_index % 2
    high = col_index // 2
    planes = col_count // 2
    super_count, shard_rows, width = panels.shape
    tile_rows = width // row_count
    tile_cols = width // col_count
    group_rows = row_count * shard_rows
    plane_rows = 2 * group_rows
    blocks = pattern.shape[0]
    assert super_count == 2 and planes == row_count and rows_here == plane_rows
    assert group_rows == cols_here == BLK and blocks == col_count
    assert 2 * shard_rows == tile_cols
    members = [
        [(2 * plane + near) * row_count + row for near in range(2) for row in range(row_count)]
        for plane in range(planes)
    ]

    held = rows_first(ancestor_inverse)

    shares = jnp.swapaxes(panels.reshape(2, shard_rows, row_count, tile_rows), 1, 2)
    shares = shares.reshape(2 * row_count, shard_rows, tile_rows)
    piece = lax.all_to_all(
        shares, ("col", "row"), 0, 0, tiled=True, axis_index_groups=members
    ).reshape(plane_rows, tile_rows)

    pieces = {0: piece}
    step = planes // 2
    while step:
        for j in list(pieces):
            pieces[j ^ step] = swap(pieces[j], 0, 2 * step)
        step //= 2
    pattern, listed, link = after(piece, pattern, listed, parent_panels[0])

    block_ids = jnp.arange(blocks, dtype=jnp.int32)
    flags = jnp.any(listed[:, :, None] == block_ids[None, None, :], axis=1).astype(jnp.float32)
    seen = lax.dynamic_slice_in_dim(pattern, 2 * high, 2, 1).astype(jnp.float32)
    seen = (seen * pick(flags, low)[:, None]).reshape(planes, 2, 2)
    total = None
    for j in sorted(pieces, key=lambda j: (bin(j).count("1"), -j)):
        source = high ^ j
        weights = [
            pick(held, row_index ^ source, low ^ near).reshape(2, BLK, cols_here)
            * pick(seen, source)[:, near][:, None, None]
            for near in range(2)
        ]
        weights = jnp.concatenate([w.reshape(plane_rows, cols_here) for w in weights], axis=1)
        term = dot(weights, pieces[j], 0, 0)
        total = term if total is None else total + term

    keep = lax.dynamic_slice_in_dim(flags, 2 * high, 2, 1)
    keep = jnp.repeat(keep, BLK, axis=1)[:, :, None]
    raw = jnp.concatenate([panels.reshape(2 * shard_rows, width), diag_inverse[0].T], axis=1)
    raw = column_first(raw)
    raw = jnp.stack([pick(raw, row_index ^ r, low ^ k) for k in range(2) for r in range(row_count)])
    diag_rows = raw[:, :, width:].reshape(2, row_count, tile_cols, tile_rows)
    diag_rows = jnp.concatenate(
        [diag_rows[:, r].reshape(2 * tile_cols, tile_rows) for r in range(row_count)], axis=1
    )
    kept_all = [
        raw[:, s * shard_rows : (s + 1) * shard_rows, :width].reshape(plane_rows, width) * keep[s]
        for s in range(2)
    ]

    def band(value):
        return lax.dynamic_slice_in_dim(value, row_index * tile_rows, tile_rows, 1)

    kept_own = [band(value) for value in kept_all]
    link_own = band(link)
    moved = dot(kept_all[0], link_own)
    link_rows = lax.dynamic_slice_in_dim(link, high * 2 * tile_cols, 2 * tile_cols, 0)
    base = dot(dot(diag_rows, link_own), link_rows, 0, 0)

    sums = direct_gather(total)
    sums = [
        jnp.concatenate([pick(sums, row_index ^ r, low ^ s) for r in range(row_count)], axis=1)
        for s in range(2)
    ]
    upper = -sums[0] * keep[0]
    chained = dot(upper, link)
    upper_next = -(sums[1] + chained) * keep[1]
    tiles = [
        dot(-kept_own[0], upper, 0, 0),
        base
        + dot(-kept_own[1], upper_next, 0, 0)
        + dot(band(chained), kept_all[1], 0, 0)
        + dot(-moved, chained, 0, 0),
    ]
    tiles = jnp.stack([tile.T for tile in tiles]).reshape(2, planes, 2, tile_cols, tile_rows)
    tiles = lax.dynamic_index_in_dim(tiles, low, 2, keepdims=False)
    reduced = lax.dynamic_index_in_dim(tiles, high, 1, keepdims=False)
    for j in range(1, planes):
        reduced = reduced + swap(
            lax.dynamic_index_in_dim(tiles, high ^ j, 1, keepdims=False), 0, 2 * j
        )
    diagonals = diag_inverse + jnp.swapaxes(reduced, 1, 2)
    first = low * group_rows + row_index * shard_rows
    own = [lax.dynamic_slice_in_dim(value, first, shard_rows, 0) for value in (upper, upper_next)]
    return jnp.stack(own), diagonals


def solution(mesh):
    return jax.shard_map(
        local,
        mesh=mesh,
        in_specs=(
            P("row", "col"),
            P(),
            P(),
            P(None, ("col", "row"), None),
            P(),
            P(None, "row", "col"),
        ),
        out_specs=(P(None, ("col", "row"), None), P(None, "row", "col")),
        check_vma=False,
    )
```

time: 340 us -> 58.2 us (0.17)
  waiting for transfers between devices: 294 us -> 18.6 us
  starting transfers between devices: 0.29 us -> 23.1 us
  between operations: 14.3 us -> 1.06 us
  blocking collectives: 8.68 us -> 0 us
  matrix products: 10.5 us -> 5.28 us
    reduce_scatter x6 -> x0, waiting for transfers between devices: 215 us -> none  [the longest x2 127 us: local(): lax.psum_scatter(row_band, 'col', scatter_dimension=1, tiled=True)]
    psum x1 -> x0, waiting for transfers between devices: 78.2 us -> none  [broadcast(): return lax.psum(kept, axis)]
    ppermute x0 -> x16, waiting for transfers between devices: none -> 18.6 us  [the longest x9 14.1 us: swap(): return lax.ppermute(value, 'col', [(i, i ^ col_step) for i in range(cols)])]
    ppermute x0 -> x16, starting transfers between devices: none -> 17.9 us  [the longest x9 13.2 us: swap(): return lax.ppermute(value, 'col', [(i, i ^ col_step) for i in range(cols)])]
    all_gather x1 -> x0, blocking collectives: 8.68 us -> none  [local(): column_slabs = lax.all_gather(kept_panels, 'row', axis=1, tiled=True)]
    all_to_all x0 -> x1, starting transfers between devices: none -> 5.2 us  [local(): lax.all_to_all(shares, ('col', 'row'), 0, 0, tiled=True, axis_index_group...]
    dot_general x9 -> x12, matrix products: 10.5 us -> 5.28 us  [dot(): lax.dot_general(left, right, (((left_dim,), (right_dim,)), ((), ())), pre...]
    unnamed x21, local copies, waits for them, and re-layouts: 6.24 us -> 1.14 us
  transfers between devices with their start and end apart: 7 -> 17, of which waited for: 7 -> 7; matrix products, arithmetic and copies ran while one was open for 2% -> 13% of each run, Pallas kernels for 0% -> 0%
where the time goes in v1:
time: 58.2 us; the launch traced here: 57.8 us
  starting transfers between devices  23.1 us (40%)
  waiting for transfers between devices  18.6 us (32%)
  local copies, waits for them, and re-layouts  5.59 us (10%)
  matrix products  5.28 us (9%)
  other arithmetic  4.17 us (7%)
  between operations  1.06 us (2%)
    ppermute x9, waiting for transfers between devices, swap(): return lax.ppermute(value, 'col', [(i, i ^ col_step) for i in range(cols)])  14.1 us
    ppermute x9, starting transfers between devices, swap(): return lax.ppermute(value, 'col', [(i, i ^ col_step) for i in range(cols)])  13.2 us
    dot_general x12, matrix products, dot(): lax.dot_general(left, right, (((left_dim,), (right_dim,)), ((), ())), pre...  5.28 us
    all_to_all x1, starting transfers between devices, local(): lax.all_to_all(shares, ('col', 'row'), 0, 0, tiled=True, axis_index_group...  5.2 us
    ppermute x6, waiting for transfers between devices, swap(): return lax.ppermute(value, 'row', [(i, i ^ row_step) for i in range(rows)])  4.52 us
    ppermute x6, starting transfers between devices, swap(): return lax.ppermute(value, 'row', [(i, i ^ row_step) for i in range(rows)])  2.96 us
    ppermute x1, starting transfers between devices, swap(): return lax.ppermute(value, ('row', 'col'), pairs)  1.73 us
  transfers between devices with their start and end apart: 17, of which 7 were waited for; matrix products, arithmetic and copies ran while one was open for 13% of the time, Pallas kernels for 0%

profile of v1, /device:TPU:0, one launch (start us, length us, event | category | flops | bytes accessed | tf_op | source)
XLA Modules:
  0.0 57.8 jit_solution(633527830447878247)
XLA Ops:
  0.7 0.9 %fusion.77 = (f32[2,32,128]{2,1,0:T(8,128)S(1)}, f32[2,32,128]{2,1,0:T(8,128)S(1)}, f32[2,32,128]{2,1,0:T(8,128)S(1)}, f32[2,32,128]{2,1,0:T(8,128)S(1)}) fusion(f32[2,32,512]{2,1,0:T(8,128)} %param.9), kind=kLoop, calls=%fused_computation.164 | loop fusion | bytes 262144 | tf_op jit(solution)/shard_map/slice
  1.6 0.7 %pad_maximum_fusion.9 = f32[2,128,128]{2,1,0:T(8,128)} fusion(f32[2,32,128]{2,1,0:T(8,128)S(1)} %get-tuple-element.56, f32[2,32,128]{2,1,0:T(8,128)S(1)} %get-tuple-element.54, f32[2,32,128]{2,1,0:T(8,128)S(1)} %get-tuple-element.55, f32[2,32,128]{2,1,0:T(8,128)S(1)} %get-tuple-element.53), kind=kLoop, calls=%fused_computation.72 | loop fusion | flops 98304 | bytes 262144 | tf_op jit(solution)/shard_map/concatenate
  2.3 5.2 %all-to-all-start = ((f32[8,32,128]{2,1,0:T(8,128)}), f32[8,32,128]{2,1,0:T(8,128)S(1)}, u32[]{:S(2)}, u32[]{:S(2)}) async-start(f32[8,32,128]{2,1,0:T(8,128)} %bitcast.12), calls=%async_computation | async-start | bytes 262144 | tf_op jit(solution)/shard_map/all_to_all | solution.py:104
  7.5 0.8 %slice_bitcast_fusion = f32[64,128]{1,0:T(8,128)S(1)} fusion(f32[2,128,64]{1,2,0:T(8,128)} %param.11), kind=kLoop, calls=%fused_computation.111 | loop fusion | bytes 65536 | tf_op jit(solution)/shard_map/transpose | solution.py:134
  8.2 0.9 %fusion.72 = (f32[1,64,640]{2,1,0:T(8,128)S(1)}, f32[64,640]{1,0:T(8,128)S(1)}) fusion(f32[64,128]{1,0:T(8,128)S(1)} %slice_bitcast_fusion, f32[64,512]{1,0:T(8,128)} %bitcast.206), kind=kLoop, calls=%fused_computation.159 | loop fusion | flops 40960 | bytes 491520 | tf_op jit(solution)/shard_map/stack | solution.py:53
  9.1 2.1 %collective-permute-start.10 = (f32[64,640]{1,0:T(8,128)S(1)}, f32[64,640]{1,0:T(8,128)S(1)}, u32[]{:S(2)}, u32[]{:S(2)}) collective-permute-start(f32[64,640]{1,0:T(8,128)S(1)} %get-tuple-element.52), channel_id=1, source_target_pairs={{0,1},{1,0},{2,3},{3,2},{4,5},{5,4},{6,7},{7,6},{8,9},{9,8},{10,11... | collective-permute-start | bytes 491528 | tf_op jit(solution)/shard_map/ppermute | solution.py:16
  11.2 1.5 %collective-permute-start = (f32[1,256,128]{2,1,0:T(8,128)S(1)}, f32[1,256,128]{2,1,0:T(8,128)S(1)}, u32[]{:S(2)}, u32[]{:S(2)}) collective-permute-start(f32[1,256,128]{2,1,0:T(8,128)S(1)} %bitcast.219), channel_id=1, source_target_pairs={{0,16},{8,24},{16,0},{24,8},{1,17},{9,25},{17,1},{25,9},{2,18},{10... | collective-permute-start | bytes 393224 | tf_op jit(solution)/shard_map/ppermute | solution.py:14
  12.7 2.6 %collective-permute-start.3 = (f32[256,128]{1,0:T(8,128)S(1)}, f32[256,128]{1,0:T(8,128)S(1)}, u32[]{:S(2)}, u32[]{:S(2)}) collective-permute-start(f32[256,128]{1,0:T(8,128)S(1)} %bitcast.207), channel_id=1, source_target_pairs={{0,4},{1,5},{2,6},{3,7},{4,0},{5,1},{6,2},{7,3},{8,12},{9,13},{10,... | collective-permute-start | bytes 393224 | tf_op jit(solution)/shard_map/ppermute | solution.py:16
  15.3 1.6 %collective-permute-start.4 = (f32[256,128]{1,0:T(8,128)S(1)}, f32[256,128]{1,0:T(8,128)S(1)}, u32[]{:S(2)}, u32[]{:S(2)}) collective-permute-start(f32[256,128]{1,0:T(8,128)S(1)} %bitcast.208), channel_id=1, source_target_pairs={{0,2},{1,3},{2,0},{3,1},{4,6},{5,7},{6,4},{7,5},{8,10},{9,11},{10,... | collective-permute-start | bytes 393224 | tf_op jit(solution)/shard_map/ppermute | solution.py:16
  18.0 0.9 %collective-permute-start.1 = (f32[2,256,128]{2,1,0:T(8,128)S(1)}, f32[2,256,128]{2,1,0:T(8,128)S(1)}, u32[]{:S(2)}, u32[]{:S(2)}) collective-permute-start(f32[2,256,128]{2,1,0:T(8,128)S(1)} %get-tuple-element.50), channel_id=1, source_target_pairs={{0,1},{1,0},{2,3},{3,2},{4,5},{5,4},{6,7},{7,6},{8,9},{9,8},{10,11... | collective-permute-start | bytes 786440 | tf_op jit(solution)/shard_map/ppermute | solution.py:16
  19.6 5.6 %collective-permute-done.1 = f32[2,256,128]{2,1,0:T(8,128)S(1)} collective-permute-done((f32[2,256,128]{2,1,0:T(8,128)S(1)}, f32[2,256,128]{2,1,0:T(8,128)S(1)}, u32[]{:S(2)}, u32[]{:S(2)}) %collective-permute-start.1) | collective-permute-done | bytes 262176 | tf_op jit(solution)/shard_map/ppermute | solution.py:16
  26.0 1.7 %collective-permute-done.11 = f32[1,2,64,640]{3,2,1,0:T(8,128)S(1)} collective-permute-done((f32[1,2,64,640]{3,2,1,0:T(8,128)S(1)}, f32[1,2,64,640]{3,2,1,0:T(8,128)S(1)}, u32[]{:S(2)}, u32[]{:S(2)}) %collective-permute-start.11) | collective-permute-done | bytes 327712 | tf_op jit(solution)/shard_map/ppermute | solution.py:14
  29.2 2.3 %collective-permute-done.5 = f32[256,128]{1,0:T(8,128)S(1)} collective-permute-done((f32[256,128]{1,0:T(8,128)S(1)}, f32[256,128]{1,0:T(8,128)S(1)}, u32[]{:S(2)}, u32[]{:S(2)}) %collective-permute-start.5) | collective-permute-done | bytes 131104 | tf_op jit(solution)/shard_map/ppermute | solution.py:16
  31.7 1.2 %collective-permute-start.6 = (f32[256,128]{0,1:T(8,128)S(1)}, f32[256,128]{0,1:T(8,128)S(1)}, u32[]{:S(2)}, u32[]{:S(2)}) collective-permute-start(f32[256,128]{0,1:T(8,128)S(1)} %convolution_add_fusion.3), channel_id=1, source_target_pairs={{0,1},{1,0},{2,3},{3,2},{4,5},{5,4},{6,7},{7,6},{8,9},{9,8},{10,11... | collective-permute-start | bytes 393224 | tf_op jit(solution)/shard_map/ppermute | solution.py:16
  32.9 0.7 %collective-permute-start.7 = (f32[256,128]{0,1:T(8,128)S(1)}, f32[256,128]{0,1:T(8,128)S(1)}, u32[]{:S(2)}, u32[]{:S(2)}) collective-permute-start(f32[256,128]{0,1:T(8,128)S(1)} %convolution_add_fusion.3), channel_id=1, source_target_pairs={{0,16},{8,24},{16,0},{24,8},{1,17},{9,25},{17,1},{25,9},{2,18},{10... | collective-permute-start | bytes 393224 | tf_op jit(solution)/shard_map/ppermute | solution.py:14
  33.6 1.7 %collective-permute-start.8 = (f32[256,128]{0,1:T(8,128)S(1)}, f32[256,128]{0,1:T(8,128)S(1)}, u32[]{:S(2)}, u32[]{:S(2)}) collective-permute-start(f32[256,128]{0,1:T(8,128)S(1)} %convolution_add_fusion.3), channel_id=1, source_target_pairs={{0,17},{1,16},{2,19},{3,18},{4,21},{5,20},{6,23},{7,22},{8,25},{9,... | collective-permute-start | bytes 393224 | tf_op jit(solution)/shard_map/ppermute | solution.py:22
  35.4 2.3 %collective-permute-done.6 = f32[256,128]{0,1:T(8,128)S(1)} collective-permute-done((f32[256,128]{0,1:T(8,128)S(1)}, f32[256,128]{0,1:T(8,128)S(1)}, u32[]{:S(2)}, u32[]{:S(2)}) %collective-permute-start.6) | collective-permute-done | bytes 131104 | tf_op jit(solution)/shard_map/ppermute | solution.py:16
  37.7 2.8 %collective-permute-done.7 = f32[256,128]{0,1:T(8,128)S(1)} collective-permute-done((f32[256,128]{0,1:T(8,128)S(1)}, f32[256,128]{0,1:T(8,128)S(1)}, u32[]{:S(2)}, u32[]{:S(2)}) %collective-permute-start.7) | collective-permute-done | bytes 131104 | tf_op jit(solution)/shard_map/ppermute | solution.py:14
  41.8 1.1 %fusion.75 = (f32[8,32,512]{2,1,0:T(8,128)}, f32[8,32,512]{2,1,0:T(8,128)}) fusion(f32[8,64,640]{2,1,0:T(8,128)S(1)} %bitcast_dynamic-update-slice_fusion), kind=kLoop, calls=%fused_computation.162 | loop fusion | bytes 2097152 | tf_op jit(solution)/shard_map/slice | solution.py:142
  43.5 0.9 %copy-done.2 = f32[8,32,512]{2,1,0:T(8,128)S(1)} copy-done((f32[8,32,512]{2,1,0:T(8,128)S(1)}, f32[8,32,512]{2,1,0:T(8,128)}, u32[]{:S(2)}) %copy-start.2) | copy-done | bytes 524312
  48.7 2.3 %collective-permute-start.14 = (f32[2,64,128]{2,1,0:T(8,128)S(1)}, f32[2,64,128]{2,1,0:T(8,128)S(1)}, u32[]{:S(2)}, u32[]{:S(2)}) collective-permute-start(f32[2,64,128]{2,1,0:T(8,128)S(1)} %get-tuple-element.38), channel_id=1, source_target_pairs={{0,4},{1,5},{2,6},{3,7},{4,0},{5,1},{6,2},{7,3},{8,12},{9,13},{10,... | collective-permute-start | bytes 196616 | tf_op jit(solution)/shard_map/ppermute | solution.py:16
  50.9 1.7 %collective-permute-start.15 = (f32[2,64,128]{2,1,0:T(8,128)S(1)}, f32[2,64,128]{2,1,0:T(8,128)S(1)}, u32[]{:S(2)}, u32[]{:S(2)}) collective-permute-start(f32[2,64,128]{2,1,0:T(8,128)S(1)} %get-tuple-element.37), channel_id=1, source_target_pairs={{0,6},{1,7},{2,4},{3,5},{4,2},{5,3},{6,0},{7,1},{8,14},{9,15},{10,... | collective-permute-start | bytes 196616 | tf_op jit(solution)/shard_map/ppermute | solution.py:16
  52.6 0.7 %pad_maximum_fusion.10 = f32[2,32,512]{2,1,0:T(8,128)} fusion(f32[1,32,512]{2,1,0:T(8,128)S(1)} %dynamic-slice_bitcast_fusion.8, f32[1,32,512]{2,1,0:T(8,128)S(1)} %dynamic-slice_bitcast_fusion.9), kind=kLoop, calls=%fused_computation.73 | loop fusion | flops 32768 | bytes 262144 | tf_op jit(solution)/shard_map/stack | solution.py:180
  53.7 3.4 %collective-permute-done.14 = f32[2,64,128]{2,1,0:T(8,128)S(1)} collective-permute-done((f32[2,64,128]{2,1,0:T(8,128)S(1)}, f32[2,64,128]{2,1,0:T(8,128)S(1)}, u32[]{:S(2)}, u32[]{:S(2)}) %collective-permute-start.14) | collective-permute-done | bytes 65568 | tf_op jit(solution)/shard_map/ppermute | solution.py:16
  (88 shorter events, 11.3 us)
Async XLA Ops:
  0.6 16.2 %copy-start = (f32[1,512,512]{2,1,0:T(8,128)S(1)}, f32[1,512,512]{2,1,0:T(8,128)}, u32[]{:S(2)}) copy-start(f32[1,512,512]{2,1,0:T(8,128)} %param.10) | copy-start | bytes 3145732
  0.6 10.6 %copy-start.4 = (f32[256,128]{1,0:T(8,128)S(1)}, f32[256,128]{1,0:T(8,128)}, u32[]{:S(2)}) copy-start(f32[256,128]{1,0:T(8,128)} %param.6) | copy-start | bytes 393220
  0.7 16.4 %copy-start.5 = (s32[8,8]{1,0:T(8,128)S(1)}, s32[8,8]{1,0:T(8,128)}, u32[]{:S(2)}) copy-start(s32[8,8]{1,0:T(8,128)} %param.7) | copy-start | bytes 772
  0.7 16.2 %copy-start.6 = (s32[2,4]{1,0:T(2,128)S(1)}, s32[2,4]{1,0:T(2,128)}, u32[]{:S(2)}) copy-start(s32[2,4]{1,0:T(2,128)} %param.8) | copy-start | bytes 100
  2.3 10.4 %all-to-all-start = ((f32[8,32,128]{2,1,0:T(8,128)}), f32[8,32,128]{2,1,0:T(8,128)S(1)}, u32[]{:S(2)}, u32[]{:S(2)}) async-start(f32[8,32,128]{2,1,0:T(8,128)} %bitcast.12), calls=%async_computation | async-start | bytes 262144 | tf_op jit(solution)/shard_map/all_to_all | solution.py:104
  9.1 9.8 %collective-permute-start.10 = (f32[64,640]{1,0:T(8,128)S(1)}, f32[64,640]{1,0:T(8,128)S(1)}, u32[]{:S(2)}, u32[]{:S(2)}) collective-permute-start(f32[64,640]{1,0:T(8,128)S(1)} %get-tuple-element.52), channel_id=1, source_target_pairs={{0,1},{1,0},{2,3},{3,2},{4,5},{5,4},{6,7},{7,6},{8,9},{9,8},{10,11... | collective-permute-start | bytes 491528 | tf_op jit(solution)/shard_map/ppermute | solution.py:16
  11.2 6.7 %collective-permute-start = (f32[1,256,128]{2,1,0:T(8,128)S(1)}, f32[1,256,128]{2,1,0:T(8,128)S(1)}, u32[]{:S(2)}, u32[]{:S(2)}) collective-permute-start(f32[1,256,128]{2,1,0:T(8,128)S(1)} %bitcast.219), channel_id=1, source_target_pairs={{0,16},{8,24},{16,0},{24,8},{1,17},{9,25},{17,1},{25,9},{2,18},{10... | collective-permute-start | bytes 393224 | tf_op jit(solution)/shard_map/ppermute | solution.py:14
  12.7 12.9 %collective-permute-start.3 = (f32[256,128]{1,0:T(8,128)S(1)}, f32[256,128]{1,0:T(8,128)S(1)}, u32[]{:S(2)}, u32[]{:S(2)}) collective-permute-start(f32[256,128]{1,0:T(8,128)S(1)} %bitcast.207), channel_id=1, source_target_pairs={{0,4},{1,5},{2,6},{3,7},{4,0},{5,1},{6,2},{7,3},{8,12},{9,13},{10,... | collective-permute-start | bytes 393224 | tf_op jit(solution)/shard_map/ppermute | solution.py:16
  15.3 13.6 %collective-permute-start.4 = (f32[256,128]{1,0:T(8,128)S(1)}, f32[256,128]{1,0:T(8,128)S(1)}, u32[]{:S(2)}, u32[]{:S(2)}) collective-permute-start(f32[256,128]{1,0:T(8,128)S(1)} %bitcast.208), channel_id=1, source_target_pairs={{0,2},{1,3},{2,0},{3,1},{4,6},{5,7},{6,4},{7,5},{8,10},{9,11},{10,... | collective-permute-start | bytes 393224 | tf_op jit(solution)/shard_map/ppermute | solution.py:16
  18.0 7.3 %collective-permute-start.1 = (f32[2,256,128]{2,1,0:T(8,128)S(1)}, f32[2,256,128]{2,1,0:T(8,128)S(1)}, u32[]{:S(2)}, u32[]{:S(2)}) collective-permute-start(f32[2,256,128]{2,1,0:T(8,128)S(1)} %get-tuple-element.50), channel_id=1, source_target_pairs={{0,1},{1,0},{2,3},{3,2},{4,5},{5,4},{6,7},{7,6},{8,9},{9,8},{10,11... | collective-permute-start | bytes 786440 | tf_op jit(solution)/shard_map/ppermute | solution.py:16
  19.0 8.7 %collective-permute-start.11 = (f32[1,2,64,640]{3,2,1,0:T(8,128)S(1)}, f32[1,2,64,640]{3,2,1,0:T(8,128)S(1)}, u32[]{:S(2)}, u32[]{:S(2)}) collective-permute-start(f32[1,2,64,640]{3,2,1,0:T(8,128)S(1)} %get-tuple-element.44), channel_id=1, source_target_pairs={{0,16},{8,24},{16,0},{24,8},{1,17},{9,25},{17,1},{25,9},{2,18},{10... | collective-permute-start | bytes 983048 | tf_op jit(solution)/shard_map/ppermute | solution.py:14
  25.3 2.5 %collective-permute-start.2 = (f32[2,2,256,128]{3,2,1,0:T(8,128)S(1)}, f32[2,2,256,128]{3,2,1,0:T(8,128)S(1)}, u32[]{:S(2)}, u32[]{:S(2)}) collective-permute-start(f32[2,2,256,128]{3,2,1,0:T(8,128)S(1)} %get-tuple-element.42), channel_id=1, source_target_pairs={{0,8},{8,0},{16,24},{24,16},{1,9},{9,1},{17,25},{25,17},{2,10},{10... | collective-permute-start | bytes 1572872 | tf_op jit(solution)/shard_map/ppermute | solution.py:14
  25.6 5.9 %collective-permute-start.5 = (f32[256,128]{1,0:T(8,128)S(1)}, f32[256,128]{1,0:T(8,128)S(1)}, u32[]{:S(2)}, u32[]{:S(2)}) collective-permute-start(f32[256,128]{1,0:T(8,128)S(1)} %collective-permute-done.3), channel_id=1, source_target_pairs={{0,2},{1,3},{2,0},{3,1},{4,6},{5,7},{6,4},{7,5},{8,10},{9,11},{10,... | collective-permute-start | bytes 393224 | tf_op jit(solution)/shard_map/ppermute | solution.py:16
  27.8 13.0 %collective-permute-start.12 = (f32[2,2,64,640]{3,2,1,0:T(8,128)S(1)}, f32[2,2,64,640]{3,2,1,0:T(8,128)S(1)}, u32[]{:S(2)}, u32[]{:S(2)}) collective-permute-start(f32[2,2,64,640]{3,2,1,0:T(8,128)S(1)} %get-tuple-element.35), channel_id=1, source_target_pairs={{0,8},{8,0},{16,24},{24,16},{1,9},{9,1},{17,25},{25,17},{2,10},{10... | collective-permute-start | bytes 1966088 | tf_op jit(solution)/shard_map/ppermute | solution.py:14
  31.7 5.9 %collective-permute-start.6 = (f32[256,128]{0,1:T(8,128)S(1)}, f32[256,128]{0,1:T(8,128)S(1)}, u32[]{:S(2)}, u32[]{:S(2)}) collective-permute-start(f32[256,128]{0,1:T(8,128)S(1)} %convolution_add_fusion.3), channel_id=1, source_target_pairs={{0,1},{1,0},{2,3},{3,2},{4,5},{5,4},{6,7},{7,6},{8,9},{9,8},{10,11... | collective-permute-start | bytes 393224 | tf_op jit(solution)/shard_map/ppermute | solution.py:16
  32.9 7.6 %collective-permute-start.7 = (f32[256,128]{0,1:T(8,128)S(1)}, f32[256,128]{0,1:T(8,128)S(1)}, u32[]{:S(2)}, u32[]{:S(2)}) collective-permute-start(f32[256,128]{0,1:T(8,128)S(1)} %convolution_add_fusion.3), channel_id=1, source_target_pairs={{0,16},{8,24},{16,0},{24,8},{1,17},{9,25},{17,1},{25,9},{2,18},{10... | collective-permute-start | bytes 393224 | tf_op jit(solution)/shard_map/ppermute | solution.py:14
  33.6 7.0 %collective-permute-start.8 = (f32[256,128]{0,1:T(8,128)S(1)}, f32[256,128]{0,1:T(8,128)S(1)}, u32[]{:S(2)}, u32[]{:S(2)}) collective-permute-start(f32[256,128]{0,1:T(8,128)S(1)} %convolution_add_fusion.3), channel_id=1, source_target_pairs={{0,17},{1,16},{2,19},{3,18},{4,21},{5,20},{6,23},{7,22},{8,25},{9,... | collective-permute-start | bytes 393224 | tf_op jit(solution)/shard_map/ppermute | solution.py:22
  40.6 2.3 %collective-permute-start.9 = (f32[2,2,256,128]{2,3,1,0:T(8,128)S(1)}, f32[2,2,256,128]{2,3,1,0:T(8,128)S(1)}, u32[]{:S(2)}, u32[]{:S(2)}) collective-permute-start(f32[2,2,256,128]{2,3,1,0:T(8,128)S(1)} %get-tuple-element.40), channel_id=1, source_target_pairs={{0,8},{8,0},{16,24},{24,16},{1,9},{9,1},{17,25},{25,17},{2,10},{10... | collective-permute-start | bytes 1572872 | tf_op jit(solution)/shard_map/ppermute | solution.py:14
  43.4 1.0 %copy-start.2 = (f32[8,32,512]{2,1,0:T(8,128)S(1)}, f32[8,32,512]{2,1,0:T(8,128)}, u32[]{:S(2)}) copy-start(f32[8,32,512]{2,1,0:T(8,128)} %get-tuple-element.17) | copy-start | bytes 1572868
  44.5 1.1 %copy-start.1 = (f32[8,32,512]{2,1,0:T(8,128)S(1)}, f32[8,32,512]{2,1,0:T(8,128)}, u32[]{:S(2)}) copy-start(f32[8,32,512]{2,1,0:T(8,128)} %get-tuple-element.16) | copy-start | bytes 1572868
  47.5 9.7 %copy-start.3 = (f32[2,128,64]{1,2,0:T(8,128)S(1)}, f32[2,128,64]{1,2,0:T(8,128)}, u32[]{:S(2)}) copy-start(f32[2,128,64]{1,2,0:T(8,128)} %param.11) | copy-start | bytes 196612
  48.2 5.5 %collective-permute-start.13 = (f32[2,64,128]{2,1,0:T(8,128)S(1)}, f32[2,64,128]{2,1,0:T(8,128)S(1)}, u32[]{:S(2)}, u32[]{:S(2)}) collective-permute-start(f32[2,64,128]{2,1,0:T(8,128)S(1)} %get-tuple-element.36), channel_id=1, source_target_pairs={{0,2},{1,3},{2,0},{3,1},{4,6},{5,7},{6,4},{7,5},{8,10},{9,11},{10,... | collective-permute-start | bytes 196616 | tf_op jit(solution)/shard_map/ppermute | solution.py:16
  48.7 8.5 %collective-permute-start.14 = (f32[2,64,128]{2,1,0:T(8,128)S(1)}, f32[2,64,128]{2,1,0:T(8,128)S(1)}, u32[]{:S(2)}, u32[]{:S(2)}) collective-permute-start(f32[2,64,128]{2,1,0:T(8,128)S(1)} %get-tuple-element.38), channel_id=1, source_target_pairs={{0,4},{1,5},{2,6},{3,7},{4,0},{5,1},{6,2},{7,3},{8,12},{9,13},{10,... | collective-permute-start | bytes 196616 | tf_op jit(solution)/shard_map/ppermute | solution.py:16
  50.9 6.2 %collective-permute-start.15 = (f32[2,64,128]{2,1,0:T(8,128)S(1)}, f32[2,64,128]{2,1,0:T(8,128)S(1)}, u32[]{:S(2)}, u32[]{:S(2)}) collective-permute-start(f32[2,64,128]{2,1,0:T(8,128)S(1)} %get-tuple-element.37), channel_id=1, source_target_pairs={{0,6},{1,7},{2,4},{3,5},{4,2},{5,3},{6,0},{7,1},{8,14},{9,15},{10,... | collective-permute-start | bytes 196616 | tf_op jit(solution)/shard_map/ppermute | solution.py:16

commit v2 on v1

--- a/solution.py
+++ b/solution.py
@@ -30,11 +30,16 @@
     return lax.optimization_barrier((value,) + others)[1:]
 
 
-def direct_gather(value):
-    rows = lax.axis_size("row")
-    far = [[swap(value, j, k) if j or k else value for k in range(2)] for j in range(0, rows, 2)]
-    far = jnp.stack([jnp.stack(pair) for pair in far])
-    return join(far, swap(far, 1, 0))
+def direct_gather(value, others):
+    rows = lax.axis_size("row")
+    far = {(0, 0): value}
+    for j in range(rows - 2, -1, -2):
+        for k in (1, 0):
+            if j or k:
+                far[j, k] = swap(value, j, k)
+    far = jnp.stack([jnp.stack([far[j, k] for k in range(2)]) for j in range(0, rows, 2)])
+    far, *others = lax.optimization_barrier((far, *others))
+    return join(far, swap(far, 1, 0)), others
 
 
 def rows_first(value):
@@ -111,22 +116,31 @@
         for j in list(pieces):
             pieces[j ^ step] = swap(pieces[j], 0, 2 * step)
         step //= 2
-    pattern, listed, link = after(piece, pattern, listed, parent_panels[0])
+    pattern, listed, link = after(pieces[planes // 2], pattern, listed, parent_panels[0])
 
     block_ids = jnp.arange(blocks, dtype=jnp.int32)
     flags = jnp.any(listed[:, :, None] == block_ids[None, None, :], axis=1).astype(jnp.float32)
     seen = lax.dynamic_slice_in_dim(pattern, 2 * high, 2, 1).astype(jnp.float32)
     seen = (seen * pick(flags, low)[:, None]).reshape(planes, 2, 2)
+    order = sorted(pieces, key=lambda j: (bin(j).count("1"), -j))
+    early = [j for j in order if bin(j).count("1") < 2]
+    late = [j for j in order if bin(j).count("1") > 1]
     total = None
-    for j in sorted(pieces, key=lambda j: (bin(j).count("1"), -j)):
-        source = high ^ j
-        weights = [
-            pick(held, row_index ^ source, low ^ near).reshape(2, BLK, cols_here)
-            * pick(seen, source)[:, near][:, None, None]
-            for near in range(2)
-        ]
-        weights = jnp.concatenate([w.reshape(plane_rows, cols_here) for w in weights], axis=1)
-        term = dot(weights, pieces[j], 0, 0)
+    for group in (early, late):
+        left = []
+        for j in group:
+            source = high ^ j
+            weights = [
+                pick(held, row_index ^ source, low ^ near).reshape(2, BLK, cols_here)
+                * pick(seen, source)[:, near][:, None, None]
+                for near in range(2)
+            ]
+            left.append(
+                jnp.concatenate([value.reshape(plane_rows, cols_here) for value in weights], axis=1)
+            )
+        left = jnp.concatenate(left, axis=0)
+        right = jnp.concatenate([pieces[j] for j in group], axis=0)
+        term = dot(left, right, 0, 0)
         total = term if total is None else total + term
 
     keep = lax.dynamic_slice_in_dim(flags, 2 * high, 2, 1)
@@ -152,7 +166,9 @@
     link_rows = lax.dynamic_slice_in_dim(link, high * 2 * tile_cols, 2 * tile_cols, 0)
     base = dot(dot(diag_rows, link_own), link_rows, 0, 0)
 
-    sums = direct_gather(total)
+    sums, (moved, base, kept_next, first_own, next_own, link) = direct_gather(
+        total, (moved, base, kept_all[1], kept_own[0], kept_own[1], link)
+    )
     sums = [
         jnp.concatenate([pick(sums, row_index ^ r, low ^ s) for r in range(row_count)], axis=1)
         for s in range(2)
@@ -161,19 +177,18 @@
     chained = dot(upper, link)
     upper_next = -(sums[1] + chained) * keep[1]
     tiles = [
-        dot(-kept_own[0], upper, 0, 0),
+        lax.optimization_barrier(dot(first_own, -upper, 0, 0)),
         base
-        + dot(-kept_own[1], upper_next, 0, 0)
-        + dot(band(chained), kept_all[1], 0, 0)
+        + dot(next_own, -upper_next, 0, 0)
+        + dot(band(chained), kept_next, 0, 0)
         + dot(-moved, chained, 0, 0),
     ]
     tiles = jnp.stack([tile.T for tile in tiles]).reshape(2, planes, 2, tile_cols, tile_rows)
     tiles = lax.dynamic_index_in_dim(tiles, low, 2, keepdims=False)
     reduced = lax.dynamic_index_in_dim(tiles, high, 1, keepdims=False)
-    for j in range(1, planes):
-        reduced = reduced + swap(
-            lax.dynamic_index_in_dim(tiles, high ^ j, 1, keepdims=False), 0, 2 * j
-        )
+    for j in range(planes - 1, 0, -1):
+        tile = lax.dynamic_index_in_dim(tiles, high ^ j, 1, keepdims=False)
+        reduced = reduced + swap(tile, 0, 2 * j)
     diagonals = diag_inverse + jnp.swapaxes(reduced, 1, 2)
     first = low * group_rows + row_index * shard_rows
     own = [lax.dynamic_slice_in_dim(value, first, shard_rows, 0) for value in (upper, upper_next)]

time: 58.2 us -> 55.7 us (0.957)
  local copies, waits for them, and re-layouts: 5.59 us -> 3.79 us
  matrix products: 5.28 us -> 4.1 us
    ppermute x6, waiting for transfers between devices: 4.52 us -> 6.3 us  [swap(): return lax.ppermute(value, 'row', [(i, i ^ row_step) for i in range(rows)])]
    ppermute x9, waiting for transfers between devices: 14.1 us -> 12.7 us  [swap(): return lax.ppermute(value, 'col', [(i, i ^ col_step) for i in range(cols)])]
    dot_general x12 -> x10, matrix products: 5.28 us -> 4.1 us  [dot(): lax.dot_general(left, right, (((left_dim,), (right_dim,)), ((), ())), pre...]
    slice x1, local copies, waits for them, and re-layouts: 1.13 us -> 0.12 us  [local(): raw[:, s * shard_rows:(s + 1) * shard_rows, :width]]
    unnamed x21 -> x17, local copies, waits for them, and re-layouts: 1.14 us -> 0.19 us
  transfers between devices with their start and end apart: 17 -> 17, of which waited for: 7 -> 9; matrix products, arithmetic and copies ran while one was open for 13% -> 10% of each run, Pallas kernels for 0% -> 0%
where the time goes in v2:
time: 55.7 us; the launch traced here: 55.4 us
  starting transfers between devices  23.2 us (42%)
  waiting for transfers between devices  19 us (34%)
  other arithmetic  4.21 us (8%)
  matrix products  4.1 us (7%)
  local copies, waits for them, and re-layouts  3.79 us (7%)
  between operations  1.1 us (2%)
    ppermute x9, starting transfers between devices, swap(): return lax.ppermute(value, 'col', [(i, i ^ col_step) for i in range(cols)])  12.9 us
    ppermute x9, waiting for transfers between devices, swap(): return lax.ppermute(value, 'col', [(i, i ^ col_step) for i in range(cols)])  12.7 us
    ppermute x6, waiting for transfers between devices, swap(): return lax.ppermute(value, 'row', [(i, i ^ row_step) for i in range(rows)])  6.3 us
    all_to_all x1, starting transfers between devices, local(): lax.all_to_all(shares, ('col', 'row'), 0, 0, tiled=True, axis_index_group...  5.2 us
    dot_general x10, matrix products, dot(): lax.dot_general(left, right, (((left_dim,), (right_dim,)), ((), ())), pre...  4.1 us
    ppermute x6, starting transfers between devices, swap(): return lax.ppermute(value, 'row', [(i, i ^ row_step) for i in range(rows)])  3.34 us
    ppermute x1, starting transfers between devices, swap(): return lax.ppermute(value, ('row', 'col'), pairs)  1.73 us
  transfers between devices with their start and end apart: 17, of which 9 were waited for; matrix products, arithmetic and copies ran while one was open for 10% of the time, Pallas kernels for 0%

profile of v2, /device:TPU:0, one launch (start us, length us, event | category | flops | bytes accessed | tf_op | source)
XLA Modules:
  0.0 55.4 jit_solution(2577147207049958682)
XLA Ops:
  0.7 0.9 %fusion.80 = (f32[2,32,128]{2,1,0:T(8,128)S(1)}, f32[2,32,128]{2,1,0:T(8,128)S(1)}, f32[2,32,128]{2,1,0:T(8,128)S(1)}, f32[2,32,128]{2,1,0:T(8,128)S(1)}) fusion(f32[2,32,512]{2,1,0:T(8,128)} %param.9), kind=kLoop, calls=%fused_computation.166 | loop fusion | bytes 262144 | tf_op jit(solution)/shard_map/slice
  1.6 0.7 %pad_maximum_fusion.9 = f32[2,128,128]{2,1,0:T(8,128)} fusion(f32[2,32,128]{2,1,0:T(8,128)S(1)} %get-tuple-element.68, f32[2,32,128]{2,1,0:T(8,128)S(1)} %get-tuple-element.66, f32[2,32,128]{2,1,0:T(8,128)S(1)} %get-tuple-element.67, f32[2,32,128]{2,1,0:T(8,128)S(1)} %get-tuple-element.65), kind=kLoop, calls=%fused_computation.81 | loop fusion | flops 98304 | bytes 262144 | tf_op jit(solution)/shard_map/concatenate
  2.3 5.2 %all-to-all-start = ((f32[8,32,128]{2,1,0:T(8,128)}), f32[8,32,128]{2,1,0:T(8,128)S(1)}, u32[]{:S(2)}, u32[]{:S(2)}) async-start(f32[8,32,128]{2,1,0:T(8,128)} %bitcast.12), calls=%async_computation | async-start | bytes 262144 | tf_op jit(solution)/shard_map/all_to_all | solution.py:109
  7.5 2.0 %collective-permute-start = (f32[1,256,128]{2,1,0:T(8,128)}, f32[1,256,128]{2,1,0:T(8,128)S(1)}, u32[]{:S(2)}, u32[]{:S(2)}) collective-permute-start(f32[1,256,128]{2,1,0:T(8,128)} %bitcast.219), channel_id=1, source_target_pairs={{0,16},{8,24},{16,0},{24,8},{1,17},{9,25},{17,1},{25,9},{2,18},{10... | collective-permute-start | bytes 393224 | tf_op jit(solution)/shard_map/ppermute | solution.py:14
  9.5 0.8 %slice_bitcast_fusion = f32[64,128]{1,0:T(8,128)S(1)} fusion(f32[2,128,64]{1,2,0:T(8,128)} %param.11), kind=kLoop, calls=%fused_computation.116 | loop fusion | bytes 65536 | tf_op jit(solution)/shard_map/transpose | solution.py:148
  10.2 0.9 %fusion.76 = (f32[1,64,640]{2,1,0:T(8,128)S(1)}, f32[64,640]{1,0:T(8,128)S(1)}) fusion(f32[64,128]{1,0:T(8,128)S(1)} %slice_bitcast_fusion, f32[64,512]{1,0:T(8,128)} %bitcast.206), kind=kLoop, calls=%fused_computation.162 | loop fusion | flops 40960 | bytes 491520 | tf_op jit(solution)/shard_map/stack | solution.py:58
  11.2 1.5 %collective-permute-start.9 = (f32[64,640]{1,0:T(8,128)S(1)}, f32[64,640]{1,0:T(8,128)S(1)}, u32[]{:S(2)}, u32[]{:S(2)}) collective-permute-start(f32[64,640]{1,0:T(8,128)S(1)} %get-tuple-element.64), channel_id=1, source_target_pairs={{0,1},{1,0},{2,3},{3,2},{4,5},{5,4},{6,7},{7,6},{8,9},{9,8},{10,11... | collective-permute-start | bytes 491528 | tf_op jit(solution)/shard_map/ppermute | solution.py:16
  12.7 2.6 %collective-permute-start.3 = (f32[256,128]{1,0:T(8,128)S(1)}, f32[256,128]{1,0:T(8,128)S(1)}, u32[]{:S(2)}, u32[]{:S(2)}) collective-permute-start(f32[256,128]{1,0:T(8,128)S(1)} %bitcast.216), channel_id=1, source_target_pairs={{0,4},{1,5},{2,6},{3,7},{4,0},{5,1},{6,2},{7,3},{8,12},{9,13},{10,... | collective-permute-start | bytes 393224 | tf_op jit(solution)/shard_map/ppermute | solution.py:16
  15.3 1.6 %collective-permute-start.4 = (f32[256,128]{1,0:T(8,128)S(1)}, f32[256,128]{1,0:T(8,128)S(1)}, u32[]{:S(2)}, u32[]{:S(2)}) collective-permute-start(f32[256,128]{1,0:T(8,128)S(1)} %bitcast.217), channel_id=1, source_target_pairs={{0,2},{1,3},{2,0},{3,1},{4,6},{5,7},{6,4},{7,5},{8,10},{9,11},{10,... | collective-permute-start | bytes 393224 | tf_op jit(solution)/shard_map/ppermute | solution.py:16
  16.9 1.1 %collective-permute-start.1 = (f32[2,256,128]{2,1,0:T(8,128)S(1)}, f32[2,256,128]{2,1,0:T(8,128)S(1)}, u32[]{:S(2)}, u32[]{:S(2)}) collective-permute-start(f32[2,256,128]{2,1,0:T(8,128)S(1)} %get-tuple-element.62), channel_id=1, source_target_pairs={{0,1},{1,0},{2,3},{3,2},{4,5},{5,4},{6,7},{7,6},{8,9},{9,8},{10,11... | collective-permute-start | bytes 786440 | tf_op jit(solution)/shard_map/ppermute | solution.py:16
  18.6 2.9 %collective-permute-done.3 = f32[256,128]{1,0:T(8,128)S(1)} collective-permute-done((f32[256,128]{1,0:T(8,128)S(1)}, f32[256,128]{1,0:T(8,128)S(1)}, u32[]{:S(2)}, u32[]{:S(2)}) %collective-permute-start.3) | collective-permute-done | bytes 131104 | tf_op jit(solution)/shard_map/ppermute | solution.py:16
  22.7 1.5 %collective-permute-done.1 = f32[2,256,128]{2,1,0:T(8,128)S(1)} collective-permute-done((f32[2,256,128]{2,1,0:T(8,128)S(1)}, f32[2,256,128]{2,1,0:T(8,128)S(1)}, u32[]{:S(2)}, u32[]{:S(2)}) %collective-permute-start.1) | collective-permute-done | bytes 262176 | tf_op jit(solution)/shard_map/ppermute | solution.py:16
  24.9 1.6 %collective-permute-done.10 = f32[1,2,64,640]{3,2,1,0:T(8,128)S(1)} collective-permute-done((f32[1,2,64,640]{3,2,1,0:T(8,128)S(1)}, f32[1,2,64,640]{3,2,1,0:T(8,128)S(1)}, u32[]{:S(2)}, u32[]{:S(2)}) %collective-permute-start.10) | collective-permute-done | bytes 327712 | tf_op jit(solution)/shard_map/ppermute | solution.py:14
  27.2 0.8 %fusion.1 = f32[256,128]{1,0:T(8,128)S(1)} fusion(f32[256,128]{1,0:T(8,128)S(1)} %get-tuple-element.42, f32[256,128]{1,0:T(8,128)S(1)} %get-tuple-element.43, f32[256,128]{1,0:T(8,128)S(1)} %get-tuple-element.44, f32[256,128]{1,0:T(8,128)S(1)} %get-tuple-element.45, f32[256,128]{1,0:T(8,128)S(1)} %get-tuple-element.46, ...), kind=kOutput, calls=%fused_computation.16 | convolution fusion | flops 152174592 | bytes 1310720 | tf_op jit(solution)/shard_map/dot_general | solution.py:73
  28.0 2.4 %collective-permute-done.5 = f32[256,128]{1,0:T(8,128)S(1)} collective-permute-done((f32[256,128]{1,0:T(8,128)S(1)}, f32[256,128]{1,0:T(8,128)S(1)}, u32[]{:S(2)}, u32[]{:S(2)}) %collective-permute-start.5) | collective-permute-done | bytes 131104 | tf_op jit(solution)/shard_map/ppermute | solution.py:16
  30.7 1.2 %collective-permute-start.6 = (f32[256,128]{1,0:T(8,128)S(1)}, f32[256,128]{1,0:T(8,128)S(1)}, u32[]{:S(2)}, u32[]{:S(2)}) collective-permute-start(f32[256,128]{1,0:T(8,128)S(1)} %convolution_add_fusion.3), channel_id=1, source_target_pairs={{0,1},{1,0},{2,3},{3,2},{4,5},{5,4},{6,7},{7,6},{8,9},{9,8},{10,11... | collective-permute-start | bytes 393224 | tf_op jit(solution)/shard_map/ppermute | solution.py:16
  32.5 1.7 %collective-permute-start.8 = (f32[256,128]{1,0:T(8,128)S(1)}, f32[256,128]{1,0:T(8,128)S(1)}, u32[]{:S(2)}, u32[]{:S(2)}) collective-permute-start(f32[256,128]{1,0:T(8,128)S(1)} %convolution_add_fusion.3), channel_id=1, source_target_pairs={{0,17},{1,16},{2,19},{3,18},{4,21},{5,20},{6,23},{7,22},{8,25},{9,... | collective-permute-start | bytes 393224 | tf_op jit(solution)/shard_map/ppermute | solution.py:22
  34.3 2.3 %collective-permute-done.6 = f32[256,128]{1,0:T(8,128)S(1)} collective-permute-done((f32[256,128]{1,0:T(8,128)S(1)}, f32[256,128]{1,0:T(8,128)S(1)}, u32[]{:S(2)}, u32[]{:S(2)}) %collective-permute-start.6) | collective-permute-done | bytes 131104 | tf_op jit(solution)/shard_map/ppermute | solution.py:16
  36.6 2.8 %collective-permute-done.7 = f32[256,128]{1,0:T(8,128)S(1)} collective-permute-done((f32[256,128]{1,0:T(8,128)S(1)}, f32[256,128]{1,0:T(8,128)S(1)}, u32[]{:S(2)}, u32[]{:S(2)}) %collective-permute-start.7) | collective-permute-done | bytes 131104 | tf_op jit(solution)/shard_map/ppermute | solution.py:14
  41.4 1.9 %collective-permute-done.12 = f32[2,2,256,128]{3,2,1,0:T(8,128)S(1)} collective-permute-done((f32[2,2,256,128]{3,2,1,0:T(8,128)S(1)}, f32[2,2,256,128]{3,2,1,0:T(8,128)S(1)}, u32[]{:S(2)}, u32[]{:S(2)}) %collective-permute-start.12) | collective-permute-done | bytes 524320 | tf_op jit(solution)/shard_map/ppermute | solution.py:14
  46.0 2.8 %collective-permute-start.13 = (f32[2,64,128]{2,1,0:T(8,128)S(1)}, f32[2,64,128]{2,1,0:T(8,128)S(1)}, u32[]{:S(2)}, u32[]{:S(2)}) collective-permute-start(f32[2,64,128]{2,1,0:T(8,128)S(1)} %get-tuple-element.50), channel_id=1, source_target_pairs={{0,6},{1,7},{2,4},{3,5},{4,2},{5,3},{6,0},{7,1},{8,14},{9,15},{10,... | collective-permute-start | bytes 196616 | tf_op jit(solution)/shard_map/ppermute | solution.py:16
  48.8 1.6 %collective-permute-start.15 = (f32[2,64,128]{2,1,0:T(8,128)S(1)}, f32[2,64,128]{2,1,0:T(8,128)S(1)}, u32[]{:S(2)}, u32[]{:S(2)}) collective-permute-start(f32[2,64,128]{2,1,0:T(8,128)S(1)} %get-tuple-element.51), channel_id=1, source_target_pairs={{0,2},{1,3},{2,0},{3,1},{4,6},{5,7},{6,4},{7,5},{8,10},{9,11},{10,... | collective-permute-start | bytes 196616 | tf_op jit(solution)/shard_map/ppermute | solution.py:16
  51.1 1.6 %collective-permute-done.13 = f32[2,64,128]{2,1,0:T(8,128)S(1)} collective-permute-done((f32[2,64,128]{2,1,0:T(8,128)S(1)}, f32[2,64,128]{2,1,0:T(8,128)S(1)}, u32[]{:S(2)}, u32[]{:S(2)}) %collective-permute-start.13) | collective-permute-done | bytes 65568 | tf_op jit(solution)/shard_map/ppermute | solution.py:16
  52.7 2.1 %collective-permute-done.14 = f32[2,64,128]{2,1,0:T(8,128)S(1)} collective-permute-done((f32[2,64,128]{2,1,0:T(8,128)S(1)}, f32[2,64,128]{2,1,0:T(8,128)S(1)}, u32[]{:S(2)}, u32[]{:S(2)}) %collective-permute-start.14) | collective-permute-done | bytes 65568 | tf_op jit(solution)/shard_map/ppermute | solution.py:16
  (88 shorter events, 9.8 us)
Async XLA Ops:
  0.6 20.9 %copy-start = (f32[1,512,512]{2,1,0:T(8,128)S(1)}, f32[1,512,512]{2,1,0:T(8,128)}, u32[]{:S(2)}) copy-start(f32[1,512,512]{2,1,0:T(8,128)} %param.10) | copy-start | bytes 3145732
  0.6 16.2 %copy-start.2 = (f32[256,128]{1,0:T(8,128)S(1)}, f32[256,128]{1,0:T(8,128)}, u32[]{:S(2)}) copy-start(f32[256,128]{1,0:T(8,128)} %param.6) | copy-start | bytes 393220
  2.3 10.4 %all-to-all-start = ((f32[8,32,128]{2,1,0:T(8,128)}), f32[8,32,128]{2,1,0:T(8,128)S(1)}, u32[]{:S(2)}, u32[]{:S(2)}) async-start(f32[8,32,128]{2,1,0:T(8,128)} %bitcast.12), calls=%async_computation | async-start | bytes 262144 | tf_op jit(solution)/shard_map/all_to_all | solution.py:109
  7.5 14.0 %copy-start.4 = (s32[2,4]{1,0:T(2,128)S(1)}, s32[2,4]{1,0:T(2,128)}, u32[]{:S(2)}) copy-start(s32[2,4]{1,0:T(2,128)} %param.8) | copy-start | bytes 100
  7.5 14.3 %copy-start.3 = (s32[8,8]{1,0:T(8,128)S(1)}, s32[8,8]{1,0:T(8,128)}, u32[]{:S(2)}) copy-start(s32[8,8]{1,0:T(8,128)} %param.7) | copy-start | bytes 772
  7.5 9.4 %collective-permute-start = (f32[1,256,128]{2,1,0:T(8,128)}, f32[1,256,128]{2,1,0:T(8,128)S(1)}, u32[]{:S(2)}, u32[]{:S(2)}) collective-permute-start(f32[1,256,128]{2,1,0:T(8,128)} %bitcast.219), channel_id=1, source_target_pairs={{0,16},{8,24},{16,0},{24,8},{1,17},{9,25},{17,1},{25,9},{2,18},{10... | collective-permute-start | bytes 393224 | tf_op jit(solution)/shard_map/ppermute | solution.py:14
  11.2 6.9 %collective-permute-start.9 = (f32[64,640]{1,0:T(8,128)S(1)}, f32[64,640]{1,0:T(8,128)S(1)}, u32[]{:S(2)}, u32[]{:S(2)}) collective-permute-start(f32[64,640]{1,0:T(8,128)S(1)} %get-tuple-element.64), channel_id=1, source_target_pairs={{0,1},{1,0},{2,3},{3,2},{4,5},{5,4},{6,7},{7,6},{8,9},{9,8},{10,11... | collective-permute-start | bytes 491528 | tf_op jit(solution)/shard_map/ppermute | solution.py:16
  12.7 8.8 %collective-permute-start.3 = (f32[256,128]{1,0:T(8,128)S(1)}, f32[256,128]{1,0:T(8,128)S(1)}, u32[]{:S(2)}, u32[]{:S(2)}) collective-permute-start(f32[256,128]{1,0:T(8,128)S(1)} %bitcast.216), channel_id=1, source_target_pairs={{0,4},{1,5},{2,6},{3,7},{4,0},{5,1},{6,2},{7,3},{8,12},{9,13},{10,... | collective-permute-start | bytes 393224 | tf_op jit(solution)/shard_map/ppermute | solution.py:16
  15.3 11.8 %collective-permute-start.4 = (f32[256,128]{1,0:T(8,128)S(1)}, f32[256,128]{1,0:T(8,128)S(1)}, u32[]{:S(2)}, u32[]{:S(2)}) collective-permute-start(f32[256,128]{1,0:T(8,128)S(1)} %bitcast.217), channel_id=1, source_target_pairs={{0,2},{1,3},{2,0},{3,1},{4,6},{5,7},{6,4},{7,5},{8,10},{9,11},{10,... | collective-permute-start | bytes 393224 | tf_op jit(solution)/shard_map/ppermute | solution.py:16
  16.9 7.3 %collective-permute-start.1 = (f32[2,256,128]{2,1,0:T(8,128)S(1)}, f32[2,256,128]{2,1,0:T(8,128)S(1)}, u32[]{:S(2)}, u32[]{:S(2)}) collective-permute-start(f32[2,256,128]{2,1,0:T(8,128)S(1)} %get-tuple-element.62), channel_id=1, source_target_pairs={{0,1},{1,0},{2,3},{3,2},{4,5},{5,4},{6,7},{7,6},{8,9},{9,8},{10,11... | collective-permute-start | bytes 786440 | tf_op jit(solution)/shard_map/ppermute | solution.py:16
  18.1 8.4 %collective-permute-start.10 = (f32[1,2,64,640]{3,2,1,0:T(8,128)S(1)}, f32[1,2,64,640]{3,2,1,0:T(8,128)S(1)}, u32[]{:S(2)}, u32[]{:S(2)}) collective-permute-start(f32[1,2,64,640]{3,2,1,0:T(8,128)S(1)} %get-tuple-element.56), channel_id=1, source_target_pairs={{0,16},{8,24},{16,0},{24,8},{1,17},{9,25},{17,1},{25,9},{2,18},{10... | collective-permute-start | bytes 983048 | tf_op jit(solution)/shard_map/ppermute | solution.py:14
  24.3 2.4 %collective-permute-start.2 = (f32[2,2,256,128]{3,2,1,0:T(8,128)S(1)}, f32[2,2,256,128]{3,2,1,0:T(8,128)S(1)}, u32[]{:S(2)}, u32[]{:S(2)}) collective-permute-start(f32[2,2,256,128]{3,2,1,0:T(8,128)S(1)} %get-tuple-element.54), channel_id=1, source_target_pairs={{0,8},{8,0},{16,24},{24,16},{1,9},{9,1},{17,25},{25,17},{2,10},{10... | collective-permute-start | bytes 1572872 | tf_op jit(solution)/shard_map/ppermute | solution.py:14
  24.4 5.9 %collective-permute-start.5 = (f32[256,128]{1,0:T(8,128)S(1)}, f32[256,128]{1,0:T(8,128)S(1)}, u32[]{:S(2)}, u32[]{:S(2)}) collective-permute-start(f32[256,128]{1,0:T(8,128)S(1)} %collective-permute-done.3), channel_id=1, source_target_pairs={{0,2},{1,3},{2,0},{3,1},{4,6},{5,7},{6,4},{7,5},{8,10},{9,11},{10,... | collective-permute-start | bytes 393224 | tf_op jit(solution)/shard_map/ppermute | solution.py:16
  26.6 12.9 %collective-permute-start.11 = (f32[2,2,64,640]{3,2,1,0:T(8,128)S(1)}, f32[2,2,64,640]{3,2,1,0:T(8,128)S(1)}, u32[]{:S(2)}, u32[]{:S(2)}) collective-permute-start(f32[2,2,64,640]{3,2,1,0:T(8,128)S(1)} %get-tuple-element.49), channel_id=1, source_target_pairs={{0,8},{8,0},{16,24},{24,16},{1,9},{9,1},{17,25},{25,17},{2,10},{10... | collective-permute-start | bytes 1966088 | tf_op jit(solution)/shard_map/ppermute | solution.py:14
  30.7 5.9 %collective-permute-start.6 = (f32[256,128]{1,0:T(8,128)S(1)}, f32[256,128]{1,0:T(8,128)S(1)}, u32[]{:S(2)}, u32[]{:S(2)}) collective-permute-start(f32[256,128]{1,0:T(8,128)S(1)} %convolution_add_fusion.3), channel_id=1, source_target_pairs={{0,1},{1,0},{2,3},{3,2},{4,5},{5,4},{6,7},{7,6},{8,9},{9,8},{10,11... | collective-permute-start | bytes 393224 | tf_op jit(solution)/shard_map/ppermute | solution.py:16
  31.9 7.6 %collective-permute-start.7 = (f32[256,128]{1,0:T(8,128)S(1)}, f32[256,128]{1,0:T(8,128)S(1)}, u32[]{:S(2)}, u32[]{:S(2)}) collective-permute-start(f32[256,128]{1,0:T(8,128)S(1)} %convolution_add_fusion.3), channel_id=1, source_target_pairs={{0,16},{8,24},{16,0},{24,8},{1,17},{9,25},{17,1},{25,9},{2,18},{10... | collective-permute-start | bytes 393224 | tf_op jit(solution)/shard_map/ppermute | solution.py:14
  32.5 7.0 %collective-permute-start.8 = (f32[256,128]{1,0:T(8,128)S(1)}, f32[256,128]{1,0:T(8,128)S(1)}, u32[]{:S(2)}, u32[]{:S(2)}) collective-permute-start(f32[256,128]{1,0:T(8,128)S(1)} %convolution_add_fusion.3), channel_id=1, source_target_pairs={{0,17},{1,16},{2,19},{3,18},{4,21},{5,20},{6,23},{7,22},{8,25},{9,... | collective-permute-start | bytes 393224 | tf_op jit(solution)/shard_map/ppermute | solution.py:22
  41.3 2.0 %collective-permute-start.12 = (f32[2,2,256,128]{3,2,1,0:T(8,128)S(1)}, f32[2,2,256,128]{3,2,1,0:T(8,128)S(1)}, u32[]{:S(2)}, u32[]{:S(2)}) collective-permute-start(f32[2,2,256,128]{3,2,1,0:T(8,128)S(1)} %pad_maximum_fusion.5), channel_id=1, source_target_pairs={{0,8},{8,0},{16,24},{24,16},{1,9},{9,1},{17,25},{25,17},{2,10},{10... | collective-permute-start | bytes 1572872 | tf_op jit(solution)/shard_map/ppermute | solution.py:14
  45.5 9.3 %copy-start.1 = (f32[2,128,64]{1,2,0:T(8,128)S(1)}, f32[2,128,64]{1,2,0:T(8,128)}, u32[]{:S(2)}) copy-start(f32[2,128,64]{1,2,0:T(8,128)} %param.11) | copy-start | bytes 196612
  46.0 6.8 %collective-permute-start.13 = (f32[2,64,128]{2,1,0:T(8,128)S(1)}, f32[2,64,128]{2,1,0:T(8,128)S(1)}, u32[]{:S(2)}, u32[]{:S(2)}) collective-permute-start(f32[2,64,128]{2,1,0:T(8,128)S(1)} %get-tuple-element.50), channel_id=1, source_target_pairs={{0,6},{1,7},{2,4},{3,5},{4,2},{5,3},{6,0},{7,1},{8,14},{9,15},{10,... | collective-permute-start | bytes 196616 | tf_op jit(solution)/shard_map/ppermute | solution.py:16
  48.8 6.0 %collective-permute-start.14 = (f32[2,64,128]{2,1,0:T(8,128)S(1)}, f32[2,64,128]{2,1,0:T(8,128)S(1)}, u32[]{:S(2)}, u32[]{:S(2)}) collective-permute-start(f32[2,64,128]{2,1,0:T(8,128)S(1)} %get-tuple-element.52), channel_id=1, source_target_pairs={{0,4},{1,5},{2,6},{3,7},{4,0},{5,1},{6,2},{7,3},{8,12},{9,13},{10,... | collective-permute-start | bytes 196616 | tf_op jit(solution)/shard_map/ppermute | solution.py:16
  48.8 6.0 %collective-permute-start.15 = (f32[2,64,128]{2,1,0:T(8,128)S(1)}, f32[2,64,128]{2,1,0:T(8,128)S(1)}, u32[]{:S(2)}, u32[]{:S(2)}) collective-permute-start(f32[2,64,128]{2,1,0:T(8,128)S(1)} %get-tuple-element.51), channel_id=1, source_target_pairs={{0,2},{1,3},{2,0},{3,1},{4,6},{5,7},{6,4},{7,5},{8,10},{9,11},{10,... | collective-permute-start | bytes 196616 | tf_op jit(solution)/shard_map/ppermute | solution.py:16
